TPU v7x, 256 devices: a whole 4x4x8 slice. The times are simulated.
256 devices in a mesh: row: 4 (over x_hi, core), col: 8 (over z), layer: 8 (over x_lo, y).
Axes of the slice: x: 4 (x_hi: 2, x_lo: 2; x = x_hi * 2 + x_lo), y: 4, z: 8, core: 2. Of those that a mesh axis runs over, the one named last changes fastest.
Arguments:
- amplitudes: float32 [12288, 16384], P(('row', 'col', 'layer')), may hold values from -6 to 6
- integrals: float32 [16384, 2048], P(('col', 'layer')), may hold values from -0.046875 to 0.046875
- pair_list: int32 [12288, 2], P(('row', 'col', 'layer')), may hold values from 0 to 199, as said below
- occupied_energy: float32 [200], replicated, may hold values from -1.5 to -0.3
- virtual_energy: float32 [2048], replicated, may hold values from 1 to 4
Outputs:
- ladder_update: float32 [12288, 2048], P(('row', 'col', 'layer'))
Inputs may be any that keep to these rules, and one draw needn't show every extreme that they name: `pair_list`: each row (i, j) holds two occupied orbital numbers with i <= j.
All inputs are finite; a program needn't handle non-finite values.
Results may differ from a plain program's by a relative error of at most 0.000071.
Values sent between devices are 32-bit elements; how exact they have to be, the bound alone decides.
No kernel may reach another device: no remote copies, remote signals or barrier semaphores. Data moves between devices by JAX's collectives and lax.ppermute only.
A program may use at most 128 MiB of HBM per device.

v0:
```python
import jax
import jax.numpy as jnp
from jax import lax
from jax.sharding import PartitionSpec as P


def energy_lookup(pair_list, occupied_energy):
    occ_index = jnp.arange(occupied_energy.shape[0], dtype=jnp.int32)
    occ_first = jnp.sum(
        jnp.where(pair_list[:, 0:1] == occ_index[None, :], occupied_energy[None, :], 0.0), axis=1
    )
    occ_second = jnp.sum(
        jnp.where(pair_list[:, 1:2] == occ_index[None, :], occupied_energy[None, :], 0.0), axis=1
    )
    return (occ_first, occ_second)


def body(amplitudes, integrals, pair_list, occupied_energy, virtual_energy):
    row_count = amplitudes.shape[0]
    col_count = lax.axis_size("col")
    integral_block = lax.all_gather(integrals, "layer", axis=0, tiled=True)
    shaped = amplitudes.reshape(row_count, col_count, amplitudes.shape[1] // col_count)
    partial_value = jnp.einsum(
        "rsk,kn->rsn",
        lax.all_to_all(shaped, "col", split_axis=1, concat_axis=1, tiled=True),
        integral_block,
        precision=lax.Precision.HIGHEST,
        preferred_element_type=jnp.float32,
    )
    returned = lax.all_to_all(partial_value, "col", split_axis=1, concat_axis=1, tiled=True)
    ladder = jnp.sum(returned, axis=1)
    occ_first, occ_second = energy_lookup(pair_list, occupied_energy)
    denominator = virtual_energy[None, :] - occ_first[:, None] - occ_second[:, None]
    return ladder / denominator


def solution(mesh):
    in_specs = (
        P(("row", "col", "layer"), None),
        P(("col", "layer"), None),
        P(("row", "col", "layer"), None),
        P(),
        P(),
    )
    out_specs = P(("row", "col", "layer"), None)
    return jax.shard_map(body, mesh=mesh, in_specs=in_specs, out_specs=out_specs, check_vma=False)
```

profile of v0, /device:TPU:1, one launch (start us, length us, event | category | flops | bytes accessed | tf_op | source)
XLA Modules:
  0.0 299.0 jit_solution(12691873429440723505)
XLA Ops:
  6.5 0.0 all-gather.2.cloned.1.call-start
  6.5 0.7 all-gather.2.cloned.1.call-update
  7.3 2.1 copy.18
  9.4 81.1 %all_to_all.10 = f32[48,8,2048]{2,0,1:T(8,128)S(1)} all-to-all(f32[48,8,2048]{2,0,1:T(8,128)S(1)} %bitcast.12), channel_id=1, replica_groups=mesh['row'=4,'col'=8,'layer'=8] {'col'}, dimensions={1} | all-to-all | bytes 6291456 | tf_op jit(solution)/shard_map/all_to_all | solution.py:25
  90.4 95.4 %all-gather.2.cloned.1.call-done = f32[2048,2048]{1,0:T(8,128)} async-done(((f32[256,2048]{1,0:T(8,128)}), f32[2048,2048]{1,0:T(8,128)}) %all-gather.2.cloned.1.call-update) | async-done | bytes 16777232 | tf_op jit(solution)/shard_map/all_gather | solution.py:21
  185.8 24.1 %fusion = f32[48,8,2048]{2,0,1:T(8,128)} fusion(f32[48,8,2048]{2,0,1:T(8,128)S(1)} %all_to_all.10, f32[2048,2048]{1,0:T(8,128)} %all-gather.2.cloned.1.call-done), kind=kOutput, calls=%fused_computation | convolution fusion | flops 19327352832 | bytes 23068672 | tf_op jit(solution)/shard_map/rsk,kn->rsn/dot_general | solution.py:23
  209.9 0.0 copy-start.2
  209.9 0.0 copy-start.1
  209.9 6.9 %all-to-all-start.1 = ((f32[48,8,2048]{2,0,1:T(8,128)}), f32[48,8,2048]{2,0,1:T(8,128)S(1)}, u32[]{:S(2)}, u32[]{:S(2)}) async-start(f32[48,8,2048]{2,0,1:T(8,128)} %fusion), calls=%async_computation.1 | async-start | bytes 6291456 | tf_op jit(solution)/shard_map/all_to_all | solution.py:30
  216.8 0.0 copy-done.2
  216.8 0.0 copy-start
  216.9 0.0 copy-done.1
  216.9 0.2 select_reduce_fusion.1
  217.0 74.0 %all-to-all-done.1 = f32[48,8,2048]{2,0,1:T(8,128)S(1)} async-done(((f32[48,8,2048]{2,0,1:T(8,128)}), f32[48,8,2048]{2,0,1:T(8,128)S(1)}, u32[]{:S(2)}, u32[]{:S(2)}) %all-to-all-start.1) | async-done | bytes 3145760 | tf_op jit(solution)/shard_map/all_to_all | solution.py:30
  291.1 0.2 reduce_sum.27
  291.3 0.0 copy-done
  291.3 0.9 subtract_divide_fusion
  (1 shorter events, 0.0 us)
Async XLA Ops:
  6.5 179.3 %all-gather.2.cloned.1.call-start = ((), (), s32[]{:S(2)}) async-start(), calls=%async_computation.2 | async-start | bytes 18874368 | tf_op jit(solution)/shard_map/all_gather | solution.py:21
  209.9 6.9 %copy-start.2 = (s32[48,2]{0,1:T(2,128)S(1)}, s32[48,2]{0,1:T(2,128)}, u32[]{:S(2)}) copy-start(s32[48,2]{0,1:T(2,128)} %param.7) | copy-start | bytes 1156
  209.9 6.9 %copy-start.1 = (f32[200]{0:T(256)S(1)}, f32[200]{0:T(256)}, u32[]{:S(2)}) copy-start(f32[200]{0:T(256)} %param.8) | copy-start | bytes 2404
  209.9 81.1 %all-to-all-start.1 = ((f32[48,8,2048]{2,0,1:T(8,128)}), f32[48,8,2048]{2,0,1:T(8,128)S(1)}, u32[]{:S(2)}, u32[]{:S(2)}) async-start(f32[48,8,2048]{2,0,1:T(8,128)} %fusion), calls=%async_computation.1 | async-start | bytes 6291456 | tf_op jit(solution)/shard_map/all_to_all | solution.py:30
  216.8 74.4 %copy-start = (f32[2048]{0:T(1024)S(1)}, f32[2048]{0:T(1024)}, u32[]{:S(2)}) copy-start(f32[2048]{0:T(1024)} %param.9) | copy-start | bytes 24580
Sparse Core Ops, SparseCore 0:
  9.1 176.6 all-gather.1
where the time goes:
time: 299 us
  waiting for transfers between devices  170 us (57%)
  blocking collectives  81.1 us (27%)
  matrix products  24.1 us (8%)
  between operations  13.4 us (4%)
  starting transfers between devices  6.88 us (2%)
    all_gather x1, waiting for transfers between devices, body(): integral_block = lax.all_gather(integrals, 'layer', axis=0, tiled=True)  95.4 us
    all_to_all x1, blocking collectives, body(): lax.all_to_all(shaped, 'col', split_axis=1, concat_axis=1, tiled=True)  81.1 us
    all_to_all x1, waiting for transfers between devices, body(): lax.all_to_all(partial_value, 'col', split_axis=1, concat_axis=1, tiled=T...  74 us
    dot_general x1, matrix products, body(): jnp.einsum('rsk,kn->rsn', lax.all_to_all(shaped, 'col', split_axis=1, con...  24.1 us
    all_to_all x1, starting transfers between devices, body(): lax.all_to_all(partial_value, 'col', split_axis=1, concat_axis=1, tiled=T...  6.88 us
  transfers between devices with their start and end apart: 2, of which 2 were waited for; matrix products, arithmetic and copies ran while one was open for 1% of the time, Pallas kernels for 0%

commit v1 on v0

--- a/solution.py
+++ b/solution.py
@@ -2,6 +2,13 @@
 import jax.numpy as jnp
 from jax import lax
 from jax.sharding import PartitionSpec as P
+from jax.lax import all_to_all, psum
+
+
+def links_plan(block_here):
+    state_now = jnp.stack(psum(1, axis_name="layer") * [block_here], axis=0)
+    y2 = all_to_all(state_now, "layer", 0, 0)
+    return jnp.concatenate(y2, axis=0)
 
 
 def energy_lookup(pair_list, occupied_energy):
@@ -18,7 +25,7 @@
 def body(amplitudes, integrals, pair_list, occupied_energy, virtual_energy):
     row_count = amplitudes.shape[0]
     col_count = lax.axis_size("col")
-    integral_block = lax.all_gather(integrals, "layer", axis=0, tiled=True)
+    integral_block = links_plan(integrals)
     shaped = amplitudes.reshape(row_count, col_count, amplitudes.shape[1] // col_count)
     partial_value = jnp.einsum(
         "rsk,kn->rsn",

time: 299 us -> 379 us (1.27); the launches traced: 299 us -> 375 us
  blocking collectives: 81.1 us -> 267 us
  waiting for transfers between devices: 170 us -> 69.8 us
  between operations: 13.4 us -> 0.06 us
  local copies, waits for them, and re-layouts: 2.11 us -> 9.95 us
    all_to_all x0 -> x1, blocking collectives: none -> 186 us  [links_plan(): y2 = all_to_all(state_now, 'layer', 0, 0)]
    all_gather x1 -> x0, waiting for transfers between devices: 95.4 us -> none  [body(): integral_block = lax.all_gather(integrals, 'layer', axis=0, tiled=True)]
    another operation x0 -> x1, local copies, waits for them, and re-layouts: none -> 7.84 us  [links_plan(): state_now = jnp.stack(psum(1, axis_name='layer') * [block_here], axis=0)]
    all_to_all x1, waiting for transfers between devices: 74 us -> 69.8 us  [body(): lax.all_to_all(partial_value, 'col', split_axis=1, concat_axis=1, tiled=T...]
  transfers between devices with their start and end apart: 2 -> 1, of which waited for: 2 -> 1; matrix products, arithmetic and copies ran while one was open for 1% -> 0% of each run, Pallas kernels for 0% -> 0%
where the time goes in v1:
time: 379 us; the launch traced here: 375 us
  blocking collectives  267 us (70%)
  waiting for transfers between devices  69.8 us (18%)
  matrix products  22.1 us (6%)
  local copies, waits for them, and re-layouts  9.95 us (3%)
  starting transfers between devices  4 us (1%)
    all_to_all x1, blocking collectives, links_plan(): y2 = all_to_all(state_now, 'layer', 0, 0)  186 us
    all_to_all x1, blocking collectives, body(): lax.all_to_all(shaped, 'col', split_axis=1, concat_axis=1, tiled=True)  81.2 us
    all_to_all x1, waiting for transfers between devices, body(): lax.all_to_all(partial_value, 'col', split_axis=1, concat_axis=1, tiled=T...  69.8 us
    dot_general x1, matrix products, body(): jnp.einsum('rsk,kn->rsn', lax.all_to_all(shaped, 'col', split_axis=1, con...  22.1 us
    another operation x1, local copies, waits for them, and re-layouts, links_plan(): state_now = jnp.stack(psum(1, axis_name='layer') * [block_here], axis=0)  7.84 us
  transfers between devices with their start and end apart: 1, of which 1 were waited for; matrix products, arithmetic and copies ran while one was open for 0% of the time, Pallas kernels for 0%

profile of v1, /device:TPU:1, one launch (start us, length us, event | category | flops | bytes accessed | tf_op | source)
XLA Modules:
  0.0 374.6 jit_solution(3521370260746397364)
XLA Ops:
  0.0 2.1 copy.18
  2.1 0.0 copy-start
  2.1 81.2 %all_to_all.15 = f32[48,8,2048]{2,0,1:T(8,128)S(1)} all-to-all(f32[48,8,2048]{2,0,1:T(8,128)S(1)} %bitcast.14), channel_id=1, replica_groups=mesh['row'=4,'col'=8,'layer'=8] {'col'}, dimensions={1} | all-to-all | bytes 6291456 | tf_op jit(solution)/shard_map/all_to_all | solution.py:32
  83.3 0.0 copy-done
  83.3 7.8 %stack.2 = f32[8,256,2048]{2,1,0:T(8,128)} broadcast(f32[256,2048]{1,0:T(8,128)S(1)} %copy-done), dimensions={1,2} | broadcast | bytes 18874368 | tf_op jit(solution)/shard_map/stack | solution.py:9
  91.2 186.2 %all_to_all.16 = f32[8,256,2048]{2,1,0:T(8,128)S(1)} all-to-all(f32[8,256,2048]{2,1,0:T(8,128)} %stack.2), channel_id=1, replica_groups=mesh['row'=4,'col'=8,'layer'=8] {'layer'}, dimensions={0} | all-to-all | bytes 33554432 | tf_op jit(solution)/shard_map/all_to_all | solution.py:10
  277.3 22.1 %fusion = f32[48,8,2048]{2,0,1:T(8,128)} fusion(f32[48,8,2048]{2,0,1:T(8,128)S(1)} %all_to_all.15, f32[2048,2048,1]{1,0,2:T(8,128)S(1)} %bitcast.13), kind=kOutput, calls=%fused_computation.8 | convolution fusion | flops 19327352832 | bytes 23068672 | tf_op jit(solution)/shard_map/rsk,kn->rsn/dot_general | solution.py:30
  299.5 0.0 copy-start.3
  299.5 0.0 copy-start.2
  299.5 4.0 %all-to-all-start.2 = ((f32[48,8,2048]{2,0,1:T(8,128)}), f32[48,8,2048]{2,0,1:T(8,128)S(1)}, u32[]{:S(2)}, u32[]{:S(2)}) async-start(f32[48,8,2048]{2,0,1:T(8,128)} %fusion), calls=%async_computation.2 | async-start | bytes 6291456 | tf_op jit(solution)/shard_map/all_to_all | solution.py:37
  303.5 0.0 copy-done.3
  303.5 0.0 copy-start.1
  303.5 0.0 copy-done.2
  303.5 0.2 select_reduce_fusion.1
  303.7 69.8 %all-to-all-done.2 = f32[48,8,2048]{2,0,1:T(8,128)S(1)} async-done(((f32[48,8,2048]{2,0,1:T(8,128)}), f32[48,8,2048]{2,0,1:T(8,128)S(1)}, u32[]{:S(2)}, u32[]{:S(2)}) %all-to-all-start.2) | async-done | bytes 3145760 | tf_op jit(solution)/shard_map/all_to_all | solution.py:37
  373.5 0.2 reduce_sum.27
  373.7 0.0 copy-done.1
  373.7 0.9 subtract_divide_fusion
  (1 shorter events, 0.0 us)
Async XLA Ops:
  2.1 81.2 %copy-start = (f32[256,2048]{1,0:T(8,128)S(1)}, f32[256,2048]{1,0:T(8,128)}, u32[]{:S(2)}) copy-start(f32[256,2048]{1,0:T(8,128)} %param.6) | copy-start | bytes 6291460
  299.5 4.0 %copy-start.3 = (s32[48,2]{0,1:T(2,128)S(1)}, s32[48,2]{0,1:T(2,128)}, u32[]{:S(2)}) copy-start(s32[48,2]{0,1:T(2,128)} %param.7) | copy-start | bytes 1156
  299.5 4.0 %copy-start.2 = (f32[200]{0:T(256)S(1)}, f32[200]{0:T(256)}, u32[]{:S(2)}) copy-start(f32[200]{0:T(256)} %param.8) | copy-start | bytes 2404
  299.5 74.0 %all-to-all-start.2 = ((f32[48,8,2048]{2,0,1:T(8,128)}), f32[48,8,2048]{2,0,1:T(8,128)S(1)}, u32[]{:S(2)}, u32[]{:S(2)}) async-start(f32[48,8,2048]{2,0,1:T(8,128)} %fusion), calls=%async_computation.2 | async-start | bytes 6291456 | tf_op jit(solution)/shard_map/all_to_all | solution.py:37
  303.5 70.2 %copy-start.1 = (f32[2048]{0:T(1024)S(1)}, f32[2048]{0:T(1024)}, u32[]{:S(2)}) copy-start(f32[2048]{0:T(1024)} %param.9) | copy-start | bytes 24580
